TPU v7x, 256 devices: a whole 4x4x8 slice. The times are simulated.
256 devices in a mesh: vox: 64 (over y, z, core), comp: 4 (over x).
Axes of the slice: x: 4, y: 4, z: 8, core: 2. Of those that a mesh axis runs over, the one named last changes fastest.
Arguments:
- data: bfloat16 [2048, 65536], P('comp', 'vox'), may hold values from -108 to 108
- projection: bfloat16 [512, 2048], P(None, 'comp'), may hold values from -0.125 to 0.125
- initial: float32 [512, 512], P('comp'), may hold values from -0.25 to 0.25
Outputs:
- unmixing: float32 [512, 512], P('comp')
- sources: bfloat16 [512, 65536], P('comp', 'vox')
All inputs are finite; a program needn't handle non-finite values.
Results may differ from a plain program's by a relative error of at most 0.008.
Values may be sent and summed in bfloat16 or wider, within the bound.
A program may use at most 64 MiB of HBM per device.

v0:
```python
import jax
import jax.numpy as jnp
from jax import lax
from jax.sharding import PartitionSpec as P

ICA_ITERS = 2
WHITEN_STEPS = 3
DECOR_STEPS = 3


def mult(left, right):
    return jnp.dot(left, right, precision=lax.Precision.HIGHEST)


def inner(left, right):
    return lax.dot_general(
        left, right, (((1,), (1,)), ((), ())), preferred_element_type=jnp.float32
    )


def whitening(covar):
    count = covar.shape[0]
    eye = jnp.eye(count, dtype=jnp.float32)
    cscale = jnp.sqrt(jnp.sum(covar * covar) + 1e-06)
    ymat = covar / cscale
    zmat = eye
    for step in range(WHITEN_STEPS):
        middle = 1.5 * eye - 0.5 * mult(zmat, ymat)
        ymat = mult(ymat, middle)
        zmat = mult(middle, zmat)
    return (zmat / jnp.sqrt(cscale)).astype(jnp.bfloat16)


def decorrelate(newer):
    gram = mult(newer, newer.T)
    newer = newer / jnp.sqrt(jnp.sqrt(jnp.sum(gram * gram) + 1e-06))
    for step in range(DECOR_STEPS):
        newer = 1.5 * newer - 0.5 * mult(mult(newer, newer.T), newer)
    return newer


def shards(data, projection, initial):
    rows_here = initial.shape[0]
    voxels = data.shape[1] * lax.axis_size("vox")
    start_row = lax.axis_index("comp") * rows_here
    reduced_rows = lax.psum_scatter(
        jnp.dot(projection, data, preferred_element_type=jnp.float32),
        "comp",
        scatter_dimension=0,
        tiled=True,
    ).astype(jnp.bfloat16)
    reduced = lax.all_gather(reduced_rows, "comp", axis=0, tiled=True)
    cov_part = inner(reduced_rows, reduced)
    cov_summed = lax.psum(cov_part, "vox")
    covar = lax.all_gather(cov_summed, "comp", axis=0, tiled=True)
    covar = covar / voxels
    whiten = whitening(covar)
    whitened = jnp.dot(whiten, reduced, preferred_element_type=jnp.float32).astype(jnp.bfloat16)
    weights = initial
    for turn in range(ICA_ITERS):
        scores = jnp.dot(weights.astype(jnp.bfloat16), whitened, preferred_element_type=jnp.float32)
        bent = jnp.tanh(scores)
        pulled = inner(bent.astype(jnp.bfloat16), whitened)
        slope = jnp.sum(1.0 - bent * bent, axis=1)
        pulled, slope = lax.psum((pulled, slope), "vox")
        newer = pulled - slope[:, None] * weights
        whole = lax.all_gather(newer, "comp", axis=0, tiled=True)
        whole = decorrelate(whole)
        weights = lax.dynamic_slice_in_dim(whole, start_row, rows_here, 0)
    sources = jnp.dot(
        weights.astype(jnp.bfloat16), whitened, preferred_element_type=jnp.float32
    ).astype(jnp.bfloat16)
    return (weights, sources)


def solution(mesh):
    return jax.shard_map(
        shards,
        mesh=mesh,
        in_specs=(P("comp", "vox"), P(None, "comp"), P("comp", None)),
        out_specs=(P("comp", None), P("comp", "vox")),
        check_vma=False,
    )
```

profile of v0, /device:TPU:1, one launch (start us, length us, event | category | flops | bytes accessed | tf_op | source)
XLA Modules:
  0.0 766.5 jit_solution(10863912530842845717)
XLA Ops:
  7.2 0.0 copy-start
  7.2 0.0 reduce-scatter.2.cloned.1.call-start
  7.2 1.2 copy-done
  8.4 3.1 fusion.26
  11.5 0.0 reduce-scatter.2.cloned.1.call-update
  11.5 0.0 all-gather.5.cloned.1.call-start
  11.6 36.1 %reduce-scatter.2.cloned.1.call-done = f32[128,1024]{1,0:T(8,128)} async-done(((f32[512,1024]{1,0:T(8,128)}), f32[128,1024]{1,0:T(8,128)}) %reduce-scatter.2.cloned.1.call-update) | async-done | bytes 524304 | tf_op jit(solution)/shard_map/reduce_scatter | solution.py:46
  47.6 1.8 convert_element_type.29
  49.4 0.0 all-gather.5.cloned.1.call-update
  49.4 0.0 all-reduce.4.cloned.1.call-start
  49.5 25.0 %all-gather.5.cloned.1.call-done = bf16[512,1024]{1,0:T(8,128)(2,1)} async-done(((bf16[128,1024]{1,0:T(8,128)(2,1)}), bf16[512,1024]{1,0:T(8,128)(2,1)}) %all-gather.5.cloned.1.call-update) | async-done | bytes 1048592 | tf_op jit(solution)/shard_map/all_gather | solution.py:52
  74.4 2.5 fusion.27
  76.9 0.0 all-reduce.4.cloned.1.call-update
  77.0 0.0 all-gather.7.cloned.1.call-start
  77.0 181.6 %all-reduce.4.cloned.1.call-done = f32[128,512]{1,0:T(8,128)} async-done(((f32[128,512]{1,0:T(8,128)}), f32[128,512]{1,0:T(8,128)}) %all-reduce.4.cloned.1.call-update) | async-done | bytes 262160 | tf_op jit(solution)/shard_map/psum | solution.py:54
  258.6 0.0 all-gather.7.cloned.1.call-update
  258.6 0.0 all-reduce.6.cloned.1.call-start
  258.7 23.3 %all-gather.7.cloned.1.call-done = f32[512,512]{1,0:T(8,128)} async-done(((f32[128,512]{1,0:T(8,128)}), f32[512,512]{1,0:T(8,128)}) %all-gather.7.cloned.1.call-update) | async-done | bytes 1048592 | tf_op jit(solution)/shard_map/all_gather | solution.py:55
  282.0 2.1 multiply_reduce_fusion
  284.8 2.3 select_subtract_fusion.2
  287.1 1.0 fusion.5
  288.1 0.2 copy-done.5
  288.3 1.9 fusion.10
  290.2 1.9 select_subtract_fusion.1
  292.1 1.8 fusion.29
  293.9 1.8 fusion.28
  295.8 1.8 select_subtract_fusion
  297.7 13.2 %fusion.4 = bf16[512,512]{1,0:T(8,128)(2,1)S(1)} fusion(f32[512,512]{1,0:T(8,128)S(1)} %select_subtract_fusion, f32[512,512]{1,0:T(8,128)S(1)} %fusion.28, f32[]{:T(128)S(6)} %sqrt.19), kind=kOutput, calls=%fused_computation.18 | convolution fusion | flops 1611137024 | bytes 2621444 | tf_op jit(solution)/shard_map/dot_general | solution.py:12
  311.0 0.7 convolution_convert_fusion
  311.7 0.2 copy-done.7
  311.9 0.5 subtract_reduce_fusion.1
  312.4 1.2 fusion.15
  313.6 0.0 all-reduce.6.cloned.1.call-update
  313.6 0.0 all-gather.9.cloned.1.call-start
  313.7 126.7 %psum.37 = f32[128]{0:T(128)S(1)} all-reduce(f32[128]{0:T(128)S(1)} %get-tuple-element.2), channel_id=1, replica_groups=mesh['vox'=64,'comp'=4] {'vox'}, use_global_device_ids=true, to_apply=%region_5.0 | all-reduce | flops 128 | bytes 1024 | tf_op jit(solution)/shard_map/psum | solution.py:65
  440.4 53.5 %all-reduce.6.cloned.1.call-done = f32[128,512]{1,0:T(8,128)} async-done(((f32[128,512]{1,0:T(8,128)}), f32[128,512]{1,0:T(8,128)}) %all-reduce.6.cloned.1.call-update) | async-done | bytes 262160 | tf_op jit(solution)/shard_map/psum | solution.py:65
  493.9 1.7 multiply_subtract_fusion.1
  495.6 0.0 all-gather.9.cloned.1.call-update
  495.6 0.0 all-reduce.8.cloned.1.call-start
  495.7 22.1 %all-gather.9.cloned.1.call-done = f32[512,512]{1,0:T(8,128)} async-done(((f32[128,512]{1,0:T(8,128)}), f32[512,512]{1,0:T(8,128)}) %all-gather.9.cloned.1.call-update) | async-done | bytes 1048592 | tf_op jit(solution)/shard_map/all_gather | solution.py:67
  517.8 4.2 fusion.6
  522.8 1.9 fusion.8
  524.7 1.9 fusion.3
  526.6 1.9 fusion.30
  528.5 1.9 fusion.2
  530.3 1.9 fusion.31
  532.2 2.8 fusion.32
  535.0 1.3 subtract_reduce_fusion
  536.4 1.2 fusion.13
  537.6 0.0 all-reduce.8.cloned.1.call-update
  537.6 0.0 all-gather.11.cloned.1.call-start
  537.6 126.9 %psum.39 = f32[128]{0:T(128)S(1)} all-reduce(f32[128]{0:T(128)S(1)} %get-tuple-element.4), channel_id=1, replica_groups=mesh['vox'=64,'comp'=4] {'vox'}, use_global_device_ids=true, to_apply=%region_9.0 | all-reduce | flops 128 | bytes 1024 | tf_op jit(solution)/shard_map/psum | solution.py:65
  664.5 53.3 %all-reduce.8.cloned.1.call-done = f32[128,512]{1,0:T(8,128)} async-done(((f32[128,512]{1,0:T(8,128)}), f32[128,512]{1,0:T(8,128)}) %all-reduce.8.cloned.1.call-update) | async-done | bytes 262160 | tf_op jit(solution)/shard_map/psum | solution.py:65
  717.8 1.8 multiply_subtract_fusion
  719.6 0.0 all-gather.11.cloned.1.call-update
  719.7 22.2 %all-gather.11.cloned.1.call-done = f32[512,512]{1,0:T(8,128)} async-done(((f32[128,512]{1,0:T(8,128)}), f32[512,512]{1,0:T(8,128)}) %all-gather.11.cloned.1.call-update) | async-done | bytes 1048592 | tf_op jit(solution)/shard_map/all_gather | solution.py:67
  741.9 4.2 fusion.7
  746.9 1.9 fusion.9
  748.8 1.9 fusion.1
  750.7 1.9 fusion.33
  752.6 1.9 fusion
  754.5 1.9 fusion.34
  756.3 1.8 fusion.35
  758.2 1.0 convolution_convert_fusion.1
  (13 shorter events, 0.1 us)
Async XLA Ops:
  7.2 1.2 copy-start
  7.2 40.5 %reduce-scatter.2.cloned.1.call-start = ((), (), s32[]{:S(2)}) async-start(), calls=%async_computation.1 | async-start | bytes 2621440 | tf_op jit(solution)/shard_map/reduce_scatter | solution.py:46
  11.5 62.9 %all-gather.5.cloned.1.call-start = ((), (), s32[]{:S(2)}) async-start(), calls=%async_computation.2 | async-start | bytes 1310720 | tf_op jit(solution)/shard_map/all_gather | solution.py:52
  49.4 209.2 %all-reduce.4.cloned.1.call-start = ((), (), s32[]{:S(2)}) async-start(), calls=%async_computation.3 | async-start | bytes 524288 | tf_op jit(solution)/shard_map/psum | solution.py:54
  77.0 205.0 %all-gather.7.cloned.1.call-start = ((), (), s32[]{:S(2)}) async-start(), calls=%async_computation.4 | async-start | bytes 1310720 | tf_op jit(solution)/shard_map/all_gather | solution.py:55
  258.6 235.2 %all-reduce.6.cloned.1.call-start = ((), (), s32[]{:S(2)}) async-start(), calls=%async_computation.5 | async-start | bytes 524288 | tf_op jit(solution)/shard_map/psum | solution.py:65
  287.1 1.2 copy-start.5
  297.7 13.2 %copy-start.4 = (bf16[512,1024]{1,0:T(8,128)(2,1)S(1)}, bf16[512,1024]{1,0:T(8,128)(2,1)}, u32[]{:S(2)}) copy-start(bf16[512,1024]{1,0:T(8,128)(2,1)} %all-gather.5.cloned.1.call-done) | copy-start | bytes 3145732
  310.9 1.0 copy-start.7
  313.6 204.2 %all-gather.9.cloned.1.call-start = ((), (), s32[]{:S(2)}) async-start(), calls=%async_computation.6 | async-start | bytes 1310720 | tf_op jit(solution)/shard_map/all_gather | solution.py:67
  495.6 222.2 %all-reduce.8.cloned.1.call-start = ((), (), s32[]{:S(2)}) async-start(), calls=%async_computation.7 | async-start | bytes 524288 | tf_op jit(solution)/shard_map/psum | solution.py:65
  517.8 5.0 copy-start.1
  537.6 204.3 %all-gather.11.cloned.1.call-start = ((), (), s32[]{:S(2)}) async-start(), calls=%async_computation.8 | async-start | bytes 1310720 | tf_op jit(solution)/shard_map/all_gather | solution.py:67
  741.9 5.0 copy-start.2
  746.9 1.9 copy-start.3
  758.2 1.0 copy-start.6
Sparse Core Ops, SparseCore 0:
  11.6 35.9 reduce-scatter.1
  50.0 24.3 all-gather.4
  78.5 180.0 all-reduce.3
  260.3 21.6 all-gather.6
  313.7 180.0 all-reduce.5
  496.1 21.6 all-gather.8
  537.7 180.0 all-reduce.7
  720.2 21.6 all-gather.10
where the time goes:
time: 777 us; the launch traced here: 766 us
  waiting for transfers between devices  417 us (54%)
  blocking collectives  254 us (33%)
  matrix products  69.2 us (9%)
  between operations  17 us (2%)
    psum x2, blocking collectives, shards(): pulled, slope = lax.psum((pulled, slope), 'vox')  254 us
    psum x1, waiting for transfers between devices, shards(): cov_summed = lax.psum(cov_part, 'vox')  182 us
    psum x2, waiting for transfers between devices, shards(): pulled, slope = lax.psum((pulled, slope), 'vox')  107 us
    dot_general x22, matrix products, mult(): return jnp.dot(left, right, precision=lax.Precision.HIGHEST)  57.7 us
    all_gather x2, waiting for transfers between devices, shards(): whole = lax.all_gather(newer, 'comp', axis=0, tiled=True)  44.4 us
    reduce_scatter x1, waiting for transfers between devices, shards(): lax.psum_scatter(jnp.dot(projection, data, preferred_element_type=jnp.flo...  36.1 us
    all_gather x1, waiting for transfers between devices, shards(): reduced = lax.all_gather(reduced_rows, 'comp', axis=0, tiled=True)  25 us
    all_gather x1, waiting for transfers between devices, shards(): covar = lax.all_gather(cov_summed, 'comp', axis=0, tiled=True)  23.3 us
  transfers between devices with their start and end apart: 8, of which 8 were waited for; matrix products, arithmetic and copies ran while one was open for 0% of the time, Pallas kernels for 0%

commit v1 on v0

v1 whole, which is shorter than its diff:
```python
import jax
import jax.numpy as jnp
from jax import lax
from jax.experimental import pallas as pl
from jax.experimental.pallas import tpu as pltpu
from jax.sharding import PartitionSpec as P

F32 = jnp.float32
BF16 = jnp.bfloat16
MESH = pl.DeviceIdType.MESH

K = 512
ROWS = 128
VOX = 1024
HALF = 512
VOXELS = 65536
ICA_ITERS = 2


def dot(a, b):
    return jnp.dot(a, b, preferred_element_type=F32)


def dot_nt(a, b):
    return lax.dot_general(a, b, (((1,), (1,)), ((), ())), preferred_element_type=F32)


def kernel(
    proj_hbm, data_hbm, init_hbm, un_ref, src_ref,
    proj, data, w, opp_s, right_s, left_s, own, ra, rb, red, wht, bent,
    pf, cs, cr, hf, hs, zr, ys, yr, full, fa, ba, bb, bc,
    ld_sem, ra_sem, rb_sem, ag_sem, xs_sem, s_sem, r_sem, zg_sem, xg_sem,
):
    v = lax.axis_index("vox")
    x = lax.axis_index("comp")
    c = lax.rem(v, 2)
    z = lax.rem(v // 2, 8)
    y = v // 16

    def dev(y_, z_, c_, x_):
        return ((y_ * 8 + z_) * 2 + c_, x_)

    def zoff(d):
        return lax.rem(z + d, 8)

    def xoff(d):
        return lax.rem(x + d, 4)

    ypeers = [y + 1 - 2 * lax.rem(y, 2), lax.rem(y + 2, 4), 3 - y]
    partner = dev(y, z, 1 - c, x)

    barrier = pltpu.get_barrier_semaphore()
    peers = [partner]
    peers += [dev(y, zoff(d), c, x) for d in range(1, 8)]
    peers += [dev(p, z, c, x) for p in ypeers]
    peers += [dev(y, z, c, xoff(d)) for d in range(1, 4)]
    for p in peers:
        pl.semaphore_signal(barrier, inc=1, device_id=p, device_id_type=MESH)

    loads = [
        pltpu.make_async_copy(proj_hbm, proj, ld_sem.at[0]),
        pltpu.make_async_copy(data_hbm, data, ld_sem.at[1]),
        pltpu.make_async_copy(init_hbm, w, ld_sem.at[2]),
    ]
    for ld in loads:
        ld.start()
    for ld in loads:
        ld.wait()

    def send(src, dst, ssem, rsem, to):
        cp = pltpu.make_async_remote_copy(
            src_ref=src, dst_ref=dst, send_sem=ssem, recv_sem=rsem,
            device_id=to, device_id_type=MESH,
        )
        cp.start()
        return cp

    def wait_for(ref, sem):
        pltpu.make_async_copy(ref, ref, sem).wait()

    def part(block):
        return dot(proj[pl.ds(pl.multiple_of(block * ROWS, ROWS), ROWS), :], data[...])

    xr, xo, xl = xoff(1), xoff(2), xoff(3)
    right, left = dev(y, z, c, xr), dev(y, z, c, xl)
    lo, hi = slice(0, HALF), slice(HALF, VOX)

    opp_s[...] = part(xo).astype(BF16)
    pl.semaphore_wait(barrier, len(peers))
    pend = []
    pend.append(send(opp_s.at[:, lo], ra.at[0], xs_sem.at[0], ra_sem.at[0], right))
    pend.append(send(opp_s.at[:, hi], ra.at[1], xs_sem.at[1], ra_sem.at[1], left))
    own[...] = part(xr)
    right_s[:, hi] = own[:, hi].astype(BF16)
    pend.append(send(right_s.at[:, hi], rb.at[0, :, hi], xs_sem.at[2], rb_sem.at[0], right))
    fa[0:ROWS, :] = own[:, lo]
    own[...] = part(xl)
    left_s[:, lo] = own[:, lo].astype(BF16)
    pend.append(send(left_s.at[:, lo], rb.at[1, :, lo], xs_sem.at[3], rb_sem.at[1], left))
    fa[ROWS:2 * ROWS, :] = own[:, hi]
    own[...] = part(x)
    wait_for(ra.at[0], ra_sem.at[0])
    right_s[:, lo] = (fa[0:ROWS, :] + ra[0].astype(F32)).astype(BF16)
    pend.append(send(right_s.at[:, lo], rb.at[0, :, lo], xs_sem.at[4], rb_sem.at[2], right))
    wait_for(ra.at[1], ra_sem.at[1])
    left_s[:, hi] = (fa[ROWS:2 * ROWS, :] + ra[1].astype(F32)).astype(BF16)
    pend.append(send(left_s.at[:, hi], rb.at[1, :, hi], xs_sem.at[5], rb_sem.at[3], left))
    wait_for(rb.at[0, :, hi], rb_sem.at[0])
    wait_for(rb.at[1, :, lo], rb_sem.at[1])
    wait_for(rb.at[0, :, lo], rb_sem.at[2])
    wait_for(rb.at[1, :, hi], rb_sem.at[3])

    def rows_of(block):
        return pl.ds(pl.multiple_of(block * ROWS, ROWS), ROWS)

    mine, rows_r, rows_l, rows_o = rows_of(x), rows_of(xr), rows_of(xl), rows_of(xo)
    red[mine, :] = (own[...] + rb[0].astype(F32) + rb[1].astype(F32)).astype(BF16)
    pend.append(send(red.at[mine, :], red.at[mine, :], xs_sem.at[6], ag_sem.at[0], right))
    pend.append(send(red.at[mine, :], red.at[mine, :], xs_sem.at[7], ag_sem.at[1], left))
    wait_for(red.at[rows_l, :], ag_sem.at[0])
    pend.append(send(red.at[rows_l, lo], red.at[rows_l, lo], xs_sem.at[8], ag_sem.at[2], right))
    wait_for(red.at[rows_r, :], ag_sem.at[1])
    pend.append(send(red.at[rows_r, hi], red.at[rows_r, hi], xs_sem.at[9], ag_sem.at[3], left))
    wait_for(red.at[rows_o, lo], ag_sem.at[2])
    wait_for(red.at[rows_o, hi], ag_sem.at[3])

    def piece_of(z_):
        return (
            pl.ds(pl.multiple_of(16 * (z_ // 2), 16), 16),
            pl.ds(pl.multiple_of(256 * lax.rem(z_, 2), 256), 256),
        )

    def half_of(x_, c_):
        return pl.ds(pl.multiple_of(x_ * ROWS + c_ * 64, 64), 64)

    def spot(x_, c_, z_):
        return (
            pl.ds(pl.multiple_of(x_ * ROWS + c_ * 64 + 16 * (z_ // 2), 16), 16),
            pl.ds(pl.multiple_of(256 * lax.rem(z_, 2), 256), 256),
        )

    def all_sum(s):
        cs[s] = pf[pl.ds(pl.multiple_of((1 - c) * 64, 64), 64), :].astype(BF16)
        send(cs.at[s], cr.at[s], s_sem.at[s, 0], r_sem.at[s, 0], partner)
        wait_for(cr.at[s], r_sem.at[s, 0])
        hf[...] = pf[pl.ds(pl.multiple_of(c * 64, 64), 64), :] + cr[s].astype(F32)
        hs[s] = hf[...].astype(BF16)
        for d in (4, 3, 5, 2, 6, 1, 7):
            to = zoff(d)
            a, b = piece_of(to)
            send(hs.at[s, a, b], zr.at[s, d - 1], s_sem.at[s, 1], r_sem.at[s, 1], dev(y, to, c, x))
        wait_for(zr.at[s], r_sem.at[s, 1])
        a, b = piece_of(z)
        acc = hf[a, b]
        for d in range(7):
            acc = acc + zr[s, d].astype(F32)
        ys[s] = acc.astype(BF16)
        for k in range(3):
            send(ys.at[s], yr.at[s, k], s_sem.at[s, 2], r_sem.at[s, 2], dev(ypeers[k], z, c, x))
        wait_for(yr.at[s], r_sem.at[s, 2])
        first = ys[s].astype(F32) + yr[s, 0].astype(F32)
        second = yr[s, 1].astype(F32) + yr[s, 2].astype(F32)
        a, b = spot(x, c, z)
        full[s, a, b] = (first + second).astype(BF16)
        for d in (4, 3, 5, 2, 6, 1, 7):
            send(full.at[s, a, b], full.at[s, a, b], s_sem.at[s, 3], zg_sem.at[s, d - 1], dev(y, zoff(d), c, x))

        def to_x(z_):
            a, b = spot(x, c, z_)
            for d in (2, 1, 3):
                send(full.at[s, a, b], full.at[s, a, b], s_sem.at[s, 4], xg_sem.at[s, d - 1], dev(y, z, c, xoff(d)))

        to_x(z)
        for d in (1, 7, 2, 6, 3, 5, 4):
            src = zoff(8 - d)
            a, b = spot(x, c, src)
            wait_for(full.at[s, a, b], zg_sem.at[s, d - 1])
            to_x(src)

        def to_partner(x_):
            h = half_of(x_, c)
            send(full.at[s, h, :], full.at[s, h, :], s_sem.at[s, 5], r_sem.at[s, 3], partner)

        to_partner(x)
        for d in (1, 3, 2):
            src = xoff(4 - d)
            wait_for(full.at[s, half_of(src, c), :], xg_sem.at[s, d - 1])
            to_partner(src)
        wait_for(full.at[s, 0:256, :], r_sem.at[s, 3])

    def sends_done(s):
        wait_for(cs.at[s], s_sem.at[s, 0])
        wait_for(zr.at[s], s_sem.at[s, 1])
        wait_for(yr.at[s], s_sem.at[s, 2])
        wait_for(zr.at[s], s_sem.at[s, 3])
        wait_for(full.at[s, 0:192, :], s_sem.at[s, 4])
        wait_for(full.at[s, 0:256, :], s_sem.at[s, 5])

    blocks = [slice(0, 256), slice(256, 512)]

    def square(ref):
        total = jnp.zeros((1, 1), F32)
        for n in blocks:
            total = total + jnp.sum(jnp.sum(ref[n, :] * ref[n, :], axis=0, keepdims=True), axis=1, keepdims=True)
        return total

    pf[...] = dot_nt(red[mine, :], red[...])
    all_sum(0)
    fa[...] = full[0].astype(F32) * (1.0 / VOXELS)
    cscale = jnp.sqrt(square(fa) + 1e-06)
    ba[...] = (fa[...] / cscale).astype(BF16)
    for n in blocks:
        fa[:, n] = 1.5 * ba[:, n].astype(F32) - 0.5 * dot(ba[...], ba[:, n])
    bb[...] = fa[...].astype(BF16)
    for n in blocks:
        bc[:, n] = (1.5 * fa[:, n] - 0.5 * dot(ba[...], bb[:, n])).astype(BF16)
    for n in blocks:
        fa[:, n] = 1.5 * fa[:, n] - 0.5 * dot(bb[...], bc[:, n])
    bb[...] = fa[...].astype(BF16)
    row = lax.broadcasted_iota(jnp.int32, (K, 256), 0)
    col = lax.broadcasted_iota(jnp.int32, (K, 256), 1)
    for i, n in enumerate(blocks):
        eye = jnp.where(row == col + 256 * i, 2.25, 0.0)
        fa[:, n] = (
            eye - 0.75 * (ba[:, n].astype(F32) + bc[:, n].astype(F32)) + 0.25 * dot(bc[...], ba[:, n])
        )
    ba[...] = fa[...].astype(BF16)
    for n in blocks:
        bc[:, n] = dot(ba[...], bb[:, n]).astype(BF16)
    inv = 1.0 / jnp.sqrt(cscale)
    for n in blocks:
        bb[:, n] = ((1.5 * fa[:, n] - 0.5 * dot(bc[...], ba[:, n])) * inv).astype(BF16)
    for j in range(4):
        n = slice(256 * j, 256 * j + 256)
        wht[:, n] = dot(bb[...], red[:, n]).astype(BF16)

    def turn(t, carry):
        s = t + 1
        weights = w[...]
        wb = weights.astype(BF16)
        slope = jnp.zeros((ROWS, 1), F32)
        for j in range(4):
            n = slice(256 * j, 256 * j + 256)
            th = jnp.tanh(dot(wb, wht[:, n]))
            bent[:, n] = th.astype(BF16)
            slope = slope + jnp.sum(1.0 - th * th, axis=1, keepdims=True)
        pf[...] = dot_nt(bent[...], wht[...]) - slope * weights
        all_sum(s)
        for n in blocks:
            fa[:, n] = dot_nt(full[s], full[s, n, :])
        norm = jnp.sqrt(square(fa) + 1e-06)
        scale = 1.0 / jnp.sqrt(norm)
        ba[...] = (fa[...] / norm).astype(BF16)
        for n in blocks:
            fa[:, n] = (1.5 * full[s, :, n].astype(F32) - 0.5 * dot(ba[...], full[s, :, n])) * scale
        bb[...] = fa[...].astype(BF16)
        for n in blocks:
            ba[:, n] = dot_nt(bb[...], bb[n, :]).astype(BF16)
        for n in blocks:
            fa[:, n] = 1.5 * fa[:, n] - 0.5 * dot(ba[...], bb[:, n])
        bb[...] = fa[...].astype(BF16)
        mixed = dot_nt(bb[mine, :], bb[...]).astype(BF16)
        w[...] = 1.5 * fa[mine, :] - 0.5 * dot(mixed, bb[...])
        return carry

    lax.fori_loop(0, ICA_ITERS, turn, 0)

    un_ref[...] = w[...]
    wb = w[...].astype(BF16)
    for j in range(4):
        n = slice(256 * j, 256 * j + 256)
        src_ref[:, n] = dot(wb, wht[:, n]).astype(BF16)

    for cp in pend:
        cp.wait_send()

    def drain(s, carry):
        sends_done(s)
        return carry

    lax.fori_loop(0, 1 + ICA_ITERS, drain, 0)


def shards(data, projection, initial):
    dma = pltpu.SemaphoreType.DMA
    stages = 1 + ICA_ITERS
    return tuple(pl.pallas_call(
        kernel,
        out_shape=(
            jax.ShapeDtypeStruct((ROWS, K), F32),
            jax.ShapeDtypeStruct((ROWS, VOX), BF16),
        ),
        in_specs=[pl.BlockSpec(memory_space=pl.ANY)] * 3,
        out_specs=[pl.BlockSpec(memory_space=pltpu.VMEM)] * 2,
        scratch_shapes=[
            pltpu.VMEM((K, 512), BF16),
            pltpu.VMEM((512, VOX), BF16),
            pltpu.VMEM((ROWS, K), F32),
            pltpu.VMEM((ROWS, VOX), BF16),
            pltpu.VMEM((ROWS, VOX), BF16),
            pltpu.VMEM((ROWS, VOX), BF16),
            pltpu.VMEM((ROWS, VOX), F32),
            pltpu.VMEM((2, ROWS, HALF), BF16),
            pltpu.VMEM((2, ROWS, VOX), BF16),
            pltpu.VMEM((K, VOX), BF16),
            pltpu.VMEM((K, VOX), BF16),
            pltpu.VMEM((ROWS, VOX), BF16),
            pltpu.VMEM((ROWS, K), F32),
            pltpu.VMEM((stages, 64, K), BF16),
            pltpu.VMEM((stages, 64, K), BF16),
            pltpu.VMEM((64, K), F32),
            pltpu.VMEM((stages, 64, K), BF16),
            pltpu.VMEM((stages, 7, 16, 256), BF16),
            pltpu.VMEM((stages, 16, 256), BF16),
            pltpu.VMEM((stages, 3, 16, 256), BF16),
            pltpu.VMEM((stages, K, K), BF16),
            pltpu.VMEM((K, K), F32),
            pltpu.VMEM((K, K), BF16),
            pltpu.VMEM((K, K), BF16),
            pltpu.VMEM((K, K), BF16),
            dma((3,)),
            dma((2,)),
            dma((4,)),
            dma((4,)),
            dma((10,)),
            dma((stages, 6)),
            dma((stages, 4)),
            dma((stages, 7)),
            dma((stages, 3)),
        ],
        compiler_params=pltpu.CompilerParams(collective_id=0, has_side_effects=True),
    )(projection, data, initial))


def solution(mesh):
    return jax.shard_map(
        shards,
        mesh=mesh,
        in_specs=(P("comp", "vox"), P(None, "comp"), P("comp", None)),
        out_specs=(P("comp", None), P("comp", "vox")),
        check_vma=False,
    )
```

time: 777 us -> 102 us (0.13); the launches traced: 766 us -> 101 us
  waiting for transfers between devices: 417 us -> 0 us
  blocking collectives: 254 us -> 0 us
  Pallas kernels: 0 us -> 98.3 us
  matrix products: 69.2 us -> 0 us
  between operations: 17 us -> 0.65 us
    psum x3 -> x0, waiting for transfers between devices: 288 us -> none  [the longest x1 182 us: shards(): cov_summed = lax.psum(cov_part, 'vox')]
    psum x2 -> x0, blocking collectives: 254 us -> none  [shards(): pulled, slope = lax.psum((pulled, slope), 'vox')]
    pallas_call x0 -> x1, Pallas kernels: none -> 98.3 us  [shards(): pl.pallas_call(kernel, out_shape=(jax.ShapeDtypeStruct((ROWS, K), F32), j...]
    all_gather x4 -> x0, waiting for transfers between devices: 92.6 us -> none  [the longest x2 44.4 us: shards(): whole = lax.all_gather(newer, 'comp', axis=0, tiled=True)]
    dot_general x30 -> x0, matrix products: 69.2 us -> none  [the longest x22 57.7 us: mult(): return jnp.dot(left, right, precision=lax.Precision.HIGHEST)]
    reduce_scatter x1 -> x0, waiting for transfers between devices: 36.1 us -> none  [shards(): lax.psum_scatter(jnp.dot(projection, data, preferred_element_type=jnp.flo...]
  transfers between devices with their start and end apart: 8 -> 0, of which waited for: 8 -> 0; matrix products, arithmetic and copies ran while one was open for 0% -> 0% of each run, Pallas kernels for 0% -> 0%
where the time goes in v1:
time: 102 us; the launch traced here: 101 us
  Pallas kernels  98.3 us (96%)
  local copies, waits for them, and re-layouts  2.42 us (2%)
    pallas_call x1, Pallas kernels, shards(): pl.pallas_call(kernel, out_shape=(jax.ShapeDtypeStruct((ROWS, K), F32), j...  98.3 us
    unnamed x4, local copies, waits for them, and re-layouts  2.42 us

profile of v1, /device:TPU:1, one launch (start us, length us, event | category | flops | bytes accessed | tf_op | source)
XLA Modules:
  0.0 101.4 jit_solution(15995083361431055892)
XLA Ops:
  0.6 98.3 %shard_map.50 = (f32[128,512]{1,0:T(8,128)}, bf16[128,1024]{1,0:T(8,128)(2,1)}) custom-call(bf16[512,512]{1,0:T(8,128)(2,1)} %proj_hbm.1, bf16[512,1024]{1,0:T(8,128)(2,1)} %data_hbm.1, f32[128,512]{1,0:T(8,128)} %init_hbm.1), custom_call_target="tpu_custom_call" | custom-call | tf_op jit(solution)/shard_map/pallas_call | solution.py:287
  99.0 0.0 copy-start
  99.0 1.7 %copy.7 = f32[128,512]{1,0:T(8,128)} copy(f32[128,512]{1,0:T(8,128)} %get-tuple-element.4) | data formatting | bytes 524288
  100.7 0.0 copy-done
  100.7 0.7 copy.8
Async XLA Ops:
  99.0 1.7 %copy-start = (bf16[128,1024]{1,0:T(8,128)(2,1)S(1)}, bf16[128,1024]{1,0:T(8,128)(2,1)}, u32[]{:S(2)}) copy-start(bf16[128,1024]{1,0:T(8,128)(2,1)} %get-tuple-element.5) | copy-start | bytes 786436

commit v2 on v1

--- a/solution.py
+++ b/solution.py
@@ -28,8 +28,8 @@
 def kernel(
     proj_hbm, data_hbm, init_hbm, un_ref, src_ref,
     proj, data, w, opp_s, right_s, left_s, own, ra, rb, red, wht, bent,
-    pf, cs, cr, hf, hs, zr, ys, yr, full, fa, ba, bb, bc,
-    ld_sem, ra_sem, rb_sem, ag_sem, xs_sem, s_sem, r_sem, zg_sem, xg_sem,
+    pf, cs, cr, hf, hs, yr, zs, zr, full, fa, ba, bb, bc,
+    ld_sem, ra_sem, rb_sem, ag_sem, xs_sem, s_sem, r_sem, g_sem,
 ):
     v = lax.axis_index("vox")
     x = lax.axis_index("comp")
@@ -40,20 +40,23 @@
     def dev(y_, z_, c_, x_):
         return ((y_ * 8 + z_) * 2 + c_, x_)
 
-    def zoff(d):
-        return lax.rem(z + d, 8)
-
     def xoff(d):
         return lax.rem(x + d, 4)
 
-    ypeers = [y + 1 - 2 * lax.rem(y, 2), lax.rem(y + 2, 4), 3 - y]
+    def yoff(d):
+        return lax.rem(y + d, 4)
+
+    def zxor(k):
+        bits = [lax.rem(z, 2), lax.rem(z // 2, 2), z // 4]
+        bits = [1 - b if (k >> i) % 2 else b for i, b in enumerate(bits)]
+        return bits[0] + 2 * bits[1] + 4 * bits[2]
+
     partner = dev(y, z, 1 - c, x)
 
     barrier = pltpu.get_barrier_semaphore()
     peers = [partner]
-    peers += [dev(y, zoff(d), c, x) for d in range(1, 8)]
-    peers += [dev(p, z, c, x) for p in ypeers]
-    peers += [dev(y, z, c, xoff(d)) for d in range(1, 4)]
+    peers += [dev(y, zxor(k), c, x) for k in range(1, 8)]
+    peers += [dev(yoff(dy), z, c, xoff(dx)) for dx in range(4) for dy in range(4) if dx or dy]
     for p in peers:
         pl.semaphore_signal(barrier, inc=1, device_id=p, device_id_type=MESH)
 
@@ -124,20 +127,14 @@
     wait_for(red.at[rows_o, lo], ag_sem.at[2])
     wait_for(red.at[rows_o, hi], ag_sem.at[3])
 
-    def piece_of(z_):
-        return (
-            pl.ds(pl.multiple_of(16 * (z_ // 2), 16), 16),
-            pl.ds(pl.multiple_of(256 * lax.rem(z_, 2), 256), 256),
-        )
-
     def half_of(x_, c_):
         return pl.ds(pl.multiple_of(x_ * ROWS + c_ * 64, 64), 64)
 
-    def spot(x_, c_, z_):
-        return (
-            pl.ds(pl.multiple_of(x_ * ROWS + c_ * 64 + 16 * (z_ // 2), 16), 16),
-            pl.ds(pl.multiple_of(256 * lax.rem(z_, 2), 256), 256),
-        )
+    def spot(x_, y_):
+        return pl.ds(pl.multiple_of(x_ * ROWS + c * 64 + y_ * 16, 16), 16)
+
+    plane = [(dx, dy) for dx in range(4) for dy in range(4) if dx or dy]
+    plane.sort(key=lambda p: min(p[0], 4 - p[0]) + min(p[1], 4 - p[1]))
 
     def all_sum(s):
         cs[s] = pf[pl.ds(pl.multiple_of((1 - c) * 64, 64), 64), :].astype(BF16)
@@ -145,56 +142,45 @@
         wait_for(cr.at[s], r_sem.at[s, 0])
         hf[...] = pf[pl.ds(pl.multiple_of(c * 64, 64), 64), :] + cr[s].astype(F32)
         hs[s] = hf[...].astype(BF16)
-        for d in (4, 3, 5, 2, 6, 1, 7):
-            to = zoff(d)
-            a, b = piece_of(to)
-            send(hs.at[s, a, b], zr.at[s, d - 1], s_sem.at[s, 1], r_sem.at[s, 1], dev(y, to, c, x))
-        wait_for(zr.at[s], r_sem.at[s, 1])
-        a, b = piece_of(z)
-        acc = hf[a, b]
-        for d in range(7):
-            acc = acc + zr[s, d].astype(F32)
-        ys[s] = acc.astype(BF16)
-        for k in range(3):
-            send(ys.at[s], yr.at[s, k], s_sem.at[s, 2], r_sem.at[s, 2], dev(ypeers[k], z, c, x))
-        wait_for(yr.at[s], r_sem.at[s, 2])
-        first = ys[s].astype(F32) + yr[s, 0].astype(F32)
-        second = yr[s, 1].astype(F32) + yr[s, 2].astype(F32)
-        a, b = spot(x, c, z)
-        full[s, a, b] = (first + second).astype(BF16)
-        for d in (4, 3, 5, 2, 6, 1, 7):
-            send(full.at[s, a, b], full.at[s, a, b], s_sem.at[s, 3], zg_sem.at[s, d - 1], dev(y, zoff(d), c, x))
-
-        def to_x(z_):
-            a, b = spot(x, c, z_)
-            for d in (2, 1, 3):
-                send(full.at[s, a, b], full.at[s, a, b], s_sem.at[s, 4], xg_sem.at[s, d - 1], dev(y, z, c, xoff(d)))
-
-        to_x(z)
-        for d in (1, 7, 2, 6, 3, 5, 4):
-            src = zoff(8 - d)
-            a, b = spot(x, c, src)
-            wait_for(full.at[s, a, b], zg_sem.at[s, d - 1])
-            to_x(src)
-
-        def to_partner(x_):
-            h = half_of(x_, c)
-            send(full.at[s, h, :], full.at[s, h, :], s_sem.at[s, 5], r_sem.at[s, 3], partner)
-
-        to_partner(x)
-        for d in (1, 3, 2):
-            src = xoff(4 - d)
-            wait_for(full.at[s, half_of(src, c), :], xg_sem.at[s, d - 1])
-            to_partner(src)
+        for d in (2, 1, 3):
+            to = yoff(d)
+            rows = pl.ds(pl.multiple_of(to * 16, 16), 16)
+            send(hs.at[s, rows, :], yr.at[s, d - 1], s_sem.at[s, 1], r_sem.at[s, 1], dev(to, z, c, x))
+        wait_for(yr.at[s], r_sem.at[s, 1])
+        acc = hf[pl.ds(pl.multiple_of(y * 16, 16), 16), :]
+        for d in range(3):
+            acc = acc + yr[s, d].astype(F32)
+        zs[s] = acc.astype(BF16)
+        for k in (4, 5, 3, 7, 2, 6, 1):
+            send(zs.at[s], zr.at[s, k - 1], s_sem.at[s, 2], r_sem.at[s, 2], dev(y, zxor(k), c, x))
+        wait_for(zr.at[s], r_sem.at[s, 2])
+        terms = [zs[s].astype(F32)] + [zr[s, k].astype(F32) for k in range(7)]
+        while len(terms) > 1:
+            terms = [a + b for a, b in zip(terms[0::2], terms[1::2])]
+        here = spot(x, y)
+        full[s, here, :] = terms[0].astype(BF16)
+        for dx, dy in reversed(plane):
+            send(
+                full.at[s, here, :], full.at[s, here, :], s_sem.at[s, 3], g_sem.at[s, dx * 4 + dy],
+                dev(yoff(dy), z, c, xoff(dx)),
+            )
+
+        def to_partner(h):
+            send(full.at[s, h, :], full.at[s, h, :], s_sem.at[s, 4], r_sem.at[s, 3], partner)
+
+        to_partner(here)
+        for dx, dy in plane:
+            there = spot(xoff(4 - dx), yoff(4 - dy))
+            wait_for(full.at[s, there, :], g_sem.at[s, dx * 4 + dy])
+            to_partner(there)
         wait_for(full.at[s, 0:256, :], r_sem.at[s, 3])
 
     def sends_done(s):
         wait_for(cs.at[s], s_sem.at[s, 0])
-        wait_for(zr.at[s], s_sem.at[s, 1])
-        wait_for(yr.at[s], s_sem.at[s, 2])
-        wait_for(zr.at[s], s_sem.at[s, 3])
-        wait_for(full.at[s, 0:192, :], s_sem.at[s, 4])
-        wait_for(full.at[s, 0:256, :], s_sem.at[s, 5])
+        wait_for(yr.at[s], s_sem.at[s, 1])
+        wait_for(zr.at[s], s_sem.at[s, 2])
+        wait_for(full.at[s, 0:240, :], s_sem.at[s, 3])
+        wait_for(full.at[s, 0:256, :], s_sem.at[s, 4])
 
     blocks = [slice(0, 256), slice(256, 512)]
 
@@ -310,9 +296,9 @@
             pltpu.VMEM((stages, 64, K), BF16),
             pltpu.VMEM((64, K), F32),
             pltpu.VMEM((stages, 64, K), BF16),
-            pltpu.VMEM((stages, 7, 16, 256), BF16),
-            pltpu.VMEM((stages, 16, 256), BF16),
-            pltpu.VMEM((stages, 3, 16, 256), BF16),
+            pltpu.VMEM((stages, 3, 16, K), BF16),
+            pltpu.VMEM((stages, 16, K), BF16),
+            pltpu.VMEM((stages, 7, 16, K), BF16),
             pltpu.VMEM((stages, K, K), BF16),
             pltpu.VMEM((K, K), F32),
             pltpu.VMEM((K, K), BF16),
@@ -323,10 +309,9 @@
             dma((4,)),
             dma((4,)),
             dma((10,)),
-            dma((stages, 6)),
+            dma((stages, 5)),
             dma((stages, 4)),
-            dma((stages, 7)),
-            dma((stages, 3)),
+            dma((stages, 16)),
         ],
         compiler_params=pltpu.CompilerParams(collective_id=0, has_side_effects=True),
     )(projection, data, initial))

time: 102 us -> 97.2 us (0.953)
  Pallas kernels: 98.3 us -> 94 us
    pallas_call x1, Pallas kernels: 98.3 us -> 94 us  [shards(): pl.pallas_call(kernel, out_shape=(jax.ShapeDtypeStruct((ROWS, K), F32), j...]
where the time goes in v2:
time: 97.2 us; the launch traced here: 97 us
  Pallas kernels  94 us (97%)
  local copies, waits for them, and re-layouts  2.42 us (2%)
    pallas_call x1, Pallas kernels, shards(): pl.pallas_call(kernel, out_shape=(jax.ShapeDtypeStruct((ROWS, K), F32), j...  94 us
    unnamed x4, local copies, waits for them, and re-layouts  2.42 us

profile of v2, /device:TPU:1, one launch (start us, length us, event | category | flops | bytes accessed | tf_op | source)
XLA Modules:
  0.0 97.0 jit_solution(13985092133734933954)
XLA Ops:
  0.6 94.0 %shard_map.50 = (f32[128,512]{1,0:T(8,128)}, bf16[128,1024]{1,0:T(8,128)(2,1)}) custom-call(bf16[512,512]{1,0:T(8,128)(2,1)} %proj_hbm.1, bf16[512,1024]{1,0:T(8,128)(2,1)} %data_hbm.1, f32[128,512]{1,0:T(8,128)} %init_hbm.1), custom_call_target="tpu_custom_call" | custom-call | tf_op jit(solution)/shard_map/pallas_call | solution.py:273
  94.6 0.0 copy-start
  94.6 1.7 %copy.7 = f32[128,512]{1,0:T(8,128)} copy(f32[128,512]{1,0:T(8,128)} %get-tuple-element.4) | data formatting | bytes 524288
  96.3 0.0 copy-done
  96.3 0.7 copy.8
Async XLA Ops:
  94.6 1.7 %copy-start = (bf16[128,1024]{1,0:T(8,128)(2,1)S(1)}, bf16[128,1024]{1,0:T(8,128)(2,1)}, u32[]{:S(2)}) copy-start(bf16[128,1024]{1,0:T(8,128)(2,1)} %get-tuple-element.5) | copy-start | bytes 786436
